TPU v7x, 512 devices: a whole 4x8x8 slice. The times are simulated.
512 devices in a mesh: cam: 128 (over y, z, core), proj: 4 (over x).
Axes of the slice: x: 4, y: 8, z: 8, core: 2. Of those that a mesh axis runs over, the one named last changes fastest.
Arguments:
- transport: bfloat16 [65536, 16384], P('cam', 'proj'), may hold values from -0.09375 to 0.09375
- test_panel: bfloat16 [16384, 32], P(('proj', 'cam')), may hold values from -6 to 6
Outputs:
- basis: float32 [65536, 32], P('cam')
- coimage: float32 [16384, 32], P(('proj', 'cam'))
All inputs are finite; a program needn't handle non-finite values.
Results may differ from a plain program's by a relative error of at most 0.0027.
Values may be sent and summed in bfloat16 or wider, within the bound.
No kernel may reach another device: no remote copies, remote signals or barrier semaphores. Data moves between devices by JAX's collectives and lax.ppermute only.
A program may use at most 64 MiB of HBM per device.

v0:
```python
import jax
import jax.numpy as jnp
from jax import lax
from jax.sharding import PartitionSpec as P

ITERS = 2


def small_gram(block):
    return jnp.dot(
        block.T, block, precision=lax.Precision.HIGHEST, preferred_element_type=jnp.float32
    )


def apply_factor(gram, block):
    lower = jnp.linalg.cholesky(gram)
    return jax.scipy.linalg.solve_triangular(lower, block.T, lower=True).T


def on_device(transport, test_panel):
    rows_here = transport.shape[0]
    total_rows = rows_here * lax.axis_size("cam")
    panel_piece = test_panel
    basis = None
    coimage = None
    for step in range(ITERS):
        partial_sketch = jnp.dot(
            transport,
            lax.all_gather(panel_piece, "cam", axis=0, tiled=True),
            preferred_element_type=jnp.float32,
        )
        sketch = lax.psum(partial_sketch, "proj")
        gram = lax.psum(small_gram(sketch), "cam") / total_rows
        basis = apply_factor(gram, sketch)
        basis_low = basis.astype(jnp.bfloat16)
        last = step + 1 == ITERS
        coimage = lax.psum_scatter(
            lax.dot_general(
                transport, basis_low, (((0,), (0,)), ((), ())), preferred_element_type=jnp.float32
            ),
            "cam",
            scatter_dimension=0,
            tiled=True,
        )
        if not last:
            panel_piece = coimage.astype(jnp.bfloat16)
    return (basis, coimage)


def solution(mesh):
    placed = (P("cam", "proj"), P(("proj", "cam"), None))
    return jax.shard_map(
        on_device,
        mesh=mesh,
        in_specs=placed,
        out_specs=(P("cam", None), P(("proj", "cam"), None)),
        check_vma=False,
    )
```

profile of v0, /device:TPU:2, one launch (start us, length us, event | category | flops | bytes accessed | tf_op | source)
XLA Modules:
  0.0 1628.0 jit_solution(12464336792124813939)
XLA Ops:
  7.2 0.0 all-reduce.3.cloned.1.call-start
  7.2 57.9 %all_gather.6 = bf16[4096,32]{1,0:T(8,128)(2,1)S(1)} all-gather(bf16[32,32]{1,0:T(8,128)(2,1)} %param.6), channel_id=1, replica_groups=mesh['cam'=128,'proj'=4] {'cam'}, dimensions={0}, use_global_device_ids=true | all-gather | bytes 264192 | tf_op jit(solution)/shard_map/all_gather | solution.py:29
  65.1 4.2 fusion.11
  69.3 0.0 all-reduce.3.cloned.1.call-update
  69.3 0.0 reduce-scatter.7.cloned.1.call-start
  69.3 46.1 %all-reduce.3.cloned.1.call-done = f32[512,32]{0,1:T(8,128)} async-done(((f32[512,32]{0,1:T(8,128)}), f32[512,32]{0,1:T(8,128)}) %all-reduce.3.cloned.1.call-update) | async-done | bytes 65552 | tf_op jit(solution)/shard_map/psum | solution.py:32
  115.4 1.1 fusion.12
  116.5 494.6 %psum.29 = f32[32,32]{0,1:T(8,128)S(1)} all-reduce(f32[32,32]{0,1:T(8,128)S(1)} %fusion.12), channel_id=1, replica_groups=mesh['cam'=128,'proj'=4] {'cam'}, use_global_device_ids=true, to_apply=%region_1.0 | all-reduce | flops 1024 | bytes 8192 | tf_op jit(solution)/shard_map/psum | solution.py:33
  611.2 0.1 copy.10
  611.2 2.9 cholesky.44
  614.2 0.6 compare_reduce_fusion.1
  614.8 0.7 fusion.3
  615.5 2.4 custom-call.6
  617.9 1.1 convolution_convert_fusion
  619.1 3.0 convolution_bitcast_fusion.1
  622.1 2.0 copy.17
  624.0 0.0 reduce-scatter.7.cloned.1.call-update
  624.1 0.0 all-reduce.5.cloned.1.call-start
  624.1 193.1 %reduce-scatter.7.cloned.1.call-done = f32[32,32]{1,0:T(8,128)} async-done(((f32[4096,32]{1,0:T(8,128)}), f32[32,32]{1,0:T(8,128)}) %reduce-scatter.7.cloned.1.call-update) | async-done | bytes 4112
  817.2 0.8 copy.18
  818.0 0.1 copy.11
  818.1 49.0 %all_gather.7 = bf16[4096,32]{1,0:T(8,128)(2,1)S(1)} all-gather(bf16[32,32]{1,0:T(8,128)(2,1)S(1)} %copy.11), channel_id=1, replica_groups=mesh['cam'=128,'proj'=4] {'cam'}, dimensions={0}, use_global_device_ids=true | all-gather | bytes 264192 | tf_op jit(solution)/shard_map/all_gather | solution.py:29
  867.1 4.2 convolution_bitcast_fusion.3
  871.3 0.0 all-reduce.5.cloned.1.call-update
  871.3 0.0 reduce-scatter.9.cloned.1.call-start
  871.3 48.4 %all-reduce.5.cloned.1.call-done = f32[512,32]{0,1:T(8,128)} async-done(((f32[512,32]{0,1:T(8,128)}), f32[512,32]{0,1:T(8,128)}) %all-reduce.5.cloned.1.call-update) | async-done | bytes 65552 | tf_op jit(solution)/shard_map/psum | solution.py:32
  919.8 1.1 fusion.13
  920.9 494.6 %psum.31 = f32[32,32]{0,1:T(8,128)S(1)} all-reduce(f32[32,32]{0,1:T(8,128)S(1)} %fusion.13), channel_id=1, replica_groups=mesh['cam'=128,'proj'=4] {'cam'}, use_global_device_ids=true, to_apply=%region_6.9 | all-reduce | flops 1024 | bytes 8192 | tf_op jit(solution)/shard_map/psum | solution.py:33
  1415.5 0.1 copy.13
  1415.6 2.9 cholesky.55
  1418.5 0.6 compare_reduce_fusion
  1419.2 0.7 fusion.4
  1419.8 2.4 custom-call.7
  1422.3 1.1 convolution_bitcast_fusion.2
  1423.4 0.0 copy-start
  1423.4 3.0 convolution_bitcast_fusion
  1426.4 2.0 copy.19
  1428.4 0.0 reduce-scatter.9.cloned.1.call-update
  1428.4 0.0 copy-done
  1428.5 193.0 %reduce-scatter.9.cloned.1.call-done = f32[32,32]{1,0:T(8,128)} async-done(((f32[4096,32]{1,0:T(8,128)}), f32[32,32]{1,0:T(8,128)}) %reduce-scatter.9.cloned.1.call-update) | async-done | bytes 4112
  (6 shorter events, 0.1 us)
Async XLA Ops:
  7.2 108.3 %all-reduce.3.cloned.1.call-start = ((), (), s32[]{:S(2)}) async-start(), calls=%async_computation.2 | async-start | bytes 131072 | tf_op jit(solution)/shard_map/psum | solution.py:32
  69.3 747.9 %reduce-scatter.7.cloned.1.call-start = ((), (), s32[]{:S(2)}) async-start(), calls=%async_computation.4 | async-start | bytes 2113536
  624.1 295.7 %all-reduce.5.cloned.1.call-start = ((), (), s32[]{:S(2)}) async-start(), calls=%async_computation.3 | async-start | bytes 131072 | tf_op jit(solution)/shard_map/psum | solution.py:32
  871.3 750.2 %reduce-scatter.9.cloned.1.call-start = ((), (), s32[]{:S(2)}) async-start(), calls=%async_computation.5 | async-start | bytes 2113536
  1423.4 5.0 copy-start
Sparse Core Ops, SparseCore 0:
  69.4 45.9 all-reduce.2
  624.2 192.9 reduce-scatter.6
  871.4 48.3 all-reduce.4
  1428.6 192.8 reduce-scatter.8
where the time goes:
time: 1630 us
  blocking collectives  1100 us (67%)
  waiting for transfers between devices  481 us (30%)
  matrix products  18.9 us (1%)
    psum x2, blocking collectives, on_device(): gram = lax.psum(small_gram(sketch), 'cam') / total_rows  989 us
    unnamed x6, waiting for transfers between devices  386 us
    all_gather x2, blocking collectives, on_device(): lax.all_gather(panel_piece, 'cam', axis=0, tiled=True)  107 us
    psum x2, waiting for transfers between devices, on_device(): sketch = lax.psum(partial_sketch, 'proj')  94.5 us
  transfers between devices with their start and end apart: 4, of which 4 were waited for; matrix products, arithmetic and copies ran while one was open for 0% of the time, Pallas kernels for 0%

commit v1 on v0

--- a/solution.py
+++ b/solution.py
@@ -26,7 +26,9 @@
     for step in range(ITERS):
         partial_sketch = jnp.dot(
             transport,
-            lax.all_gather(panel_piece, "cam", axis=0, tiled=True),
+            jnp.concatenate(
+                lax.all_to_all(jnp.stack([panel_piece] * lax.axis_size("cam")), "cam", 0, 0), axis=0
+            ),
             preferred_element_type=jnp.float32,
         )
         sketch = lax.psum(partial_sketch, "proj")

time: 1630 us -> 1570 us (0.963)
  blocking collectives: 1100 us -> 1050 us
    all_gather x2 -> x0, blocking collectives: 107 us -> none  [on_device(): lax.all_gather(panel_piece, 'cam', axis=0, tiled=True)]
    all_to_all x0 -> x2, blocking collectives: none -> 57.9 us  [on_device(): lax.all_to_all(jnp.stack([panel_piece] * lax.axis_size('cam')), 'cam', 0, 0)]
where the time goes in v1:
time: 1570 us
  blocking collectives  1050 us (67%)
  waiting for transfers between devices  472 us (30%)
  matrix products  18.9 us (1%)
    psum x2, blocking collectives, on_device(): gram = lax.psum(small_gram(sketch), 'cam') / total_rows  989 us
    unnamed x6, waiting for transfers between devices  386 us
    psum x2, waiting for transfers between devices, on_device(): sketch = lax.psum(partial_sketch, 'proj')  85.3 us
    all_to_all x2, blocking collectives, on_device(): lax.all_to_all(jnp.stack([panel_piece] * lax.axis_size('cam')), 'cam', 0, 0)  57.9 us
  transfers between devices with their start and end apart: 4, of which 4 were waited for; matrix products, arithmetic and copies ran while one was open for 0% of the time, Pallas kernels for 0%

profile of v1, /device:TPU:2, one launch (start us, length us, event | category | flops | bytes accessed | tf_op | source)
XLA Modules:
  0.0 1573.5 jit_solution(11671873639737771188)
XLA Ops:
  7.2 0.0 all-reduce.3.cloned.1.call-start
  7.2 0.8 stack.4
  8.0 0.8 reshape.28
  8.9 32.7 %all_to_all.10 = bf16[128,2,512]{2,1,0:T(2,128)(2,1)S(1)} all-to-all(bf16[128,2,512]{2,1,0:T(2,128)(2,1)S(1)} %reshape.28), channel_id=1, replica_groups=mesh['cam'=128,'proj'=4] {'cam'}, dimensions={0} | all-to-all | bytes 524288 | tf_op jit(solution)/shard_map/all_to_all | solution.py:30
  41.6 0.5 reshape.29
  42.1 4.2 fusion.11
  46.3 0.0 all-reduce.3.cloned.1.call-update
  46.3 0.0 reduce-scatter.7.cloned.1.call-start
  46.4 42.7 %all-reduce.3.cloned.1.call-done = f32[512,32]{0,1:T(8,128)} async-done(((f32[512,32]{0,1:T(8,128)}), f32[512,32]{0,1:T(8,128)}) %all-reduce.3.cloned.1.call-update) | async-done | bytes 65552 | tf_op jit(solution)/shard_map/psum | solution.py:34
  89.0 1.1 fusion.12
  90.1 494.6 %psum.29 = f32[32,32]{0,1:T(8,128)S(1)} all-reduce(f32[32,32]{0,1:T(8,128)S(1)} %fusion.12), channel_id=1, replica_groups=mesh['cam'=128,'proj'=4] {'cam'}, use_global_device_ids=true, to_apply=%region_1.0 | all-reduce | flops 1024 | bytes 8192 | tf_op jit(solution)/shard_map/psum | solution.py:35
  584.8 0.1 copy.11
  584.8 2.9 cholesky.44
  587.8 0.6 compare_reduce_fusion.1
  588.4 0.7 fusion.3
  589.1 2.4 custom-call.6
  591.5 1.1 convolution_convert_fusion
  592.7 3.0 convolution_bitcast_fusion.1
  595.7 2.0 copy.18
  597.6 0.0 reduce-scatter.7.cloned.1.call-update
  597.7 0.0 all-reduce.5.cloned.1.call-start
  597.7 193.1 %reduce-scatter.7.cloned.1.call-done = f32[32,32]{1,0:T(8,128)} async-done(((f32[4096,32]{1,0:T(8,128)}), f32[32,32]{1,0:T(8,128)}) %reduce-scatter.7.cloned.1.call-update) | async-done | bytes 4112
  790.8 0.8 copy.19
  791.6 0.1 copy.12
  791.7 0.1 stack.5
  791.8 0.8 reshape.30
  792.6 25.2 %all_to_all.11 = bf16[128,2,512]{2,1,0:T(2,128)(2,1)S(1)} all-to-all(bf16[128,2,512]{2,1,0:T(2,128)(2,1)S(1)} %reshape.30), channel_id=1, replica_groups=mesh['cam'=128,'proj'=4] {'cam'}, dimensions={0} | all-to-all | bytes 524288 | tf_op jit(solution)/shard_map/all_to_all | solution.py:30
  817.8 0.5 reshape.31
  818.3 4.2 convolution_bitcast_fusion.3
  822.5 0.0 all-reduce.5.cloned.1.call-update
  822.6 0.0 reduce-scatter.9.cloned.1.call-start
  822.6 42.6 %all-reduce.5.cloned.1.call-done = f32[512,32]{0,1:T(8,128)} async-done(((f32[512,32]{0,1:T(8,128)}), f32[512,32]{0,1:T(8,128)}) %all-reduce.5.cloned.1.call-update) | async-done | bytes 65552 | tf_op jit(solution)/shard_map/psum | solution.py:34
  865.3 1.1 fusion.13
  866.4 494.6 %psum.31 = f32[32,32]{0,1:T(8,128)S(1)} all-reduce(f32[32,32]{0,1:T(8,128)S(1)} %fusion.13), channel_id=1, replica_groups=mesh['cam'=128,'proj'=4] {'cam'}, use_global_device_ids=true, to_apply=%region_6.9 | all-reduce | flops 1024 | bytes 8192 | tf_op jit(solution)/shard_map/psum | solution.py:35
  1361.0 0.1 copy.14
  1361.1 2.9 cholesky.55
  1364.0 0.6 compare_reduce_fusion
  1364.7 0.7 fusion.4
  1365.3 2.4 custom-call.7
  1367.8 1.1 convolution_bitcast_fusion.2
  1368.9 0.0 copy-start
  1368.9 3.0 convolution_bitcast_fusion
  1371.9 2.0 copy.20
  1373.9 0.0 reduce-scatter.9.cloned.1.call-update
  1373.9 0.0 copy-done
  1373.9 193.0 %reduce-scatter.9.cloned.1.call-done = f32[32,32]{1,0:T(8,128)} async-done(((f32[4096,32]{1,0:T(8,128)}), f32[32,32]{1,0:T(8,128)}) %reduce-scatter.9.cloned.1.call-update) | async-done | bytes 4112
  (6 shorter events, 0.1 us)
Async XLA Ops:
  7.2 81.9 %all-reduce.3.cloned.1.call-start = ((), (), s32[]{:S(2)}) async-start(), calls=%async_computation.4 | async-start | bytes 131072 | tf_op jit(solution)/shard_map/psum | solution.py:34
  46.3 744.5 %reduce-scatter.7.cloned.1.call-start = ((), (), s32[]{:S(2)}) async-start(), calls=%async_computation.6 | async-start | bytes 2113536
  597.7 267.6 %all-reduce.5.cloned.1.call-start = ((), (), s32[]{:S(2)}) async-start(), calls=%async_computation.5 | async-start | bytes 131072 | tf_op jit(solution)/shard_map/psum | solution.py:34
  822.6 744.4 %reduce-scatter.9.cloned.1.call-start = ((), (), s32[]{:S(2)}) async-start(), calls=%async_computation.7 | async-start | bytes 2113536
  1368.9 5.0 copy-start
Sparse Core Ops, SparseCore 0:
  46.4 42.5 all-reduce.2
  597.8 192.9 reduce-scatter.6
  822.7 42.5 all-reduce.4
  1374.1 192.8 reduce-scatter.8

commit v2 on v0

--- a/solution.py
+++ b/solution.py
@@ -29,7 +29,7 @@
             lax.all_gather(panel_piece, "cam", axis=0, tiled=True),
             preferred_element_type=jnp.float32,
         )
-        sketch = lax.psum(partial_sketch, "proj")
+        sketch = jnp.sum(lax.all_gather(partial_sketch, "proj"), axis=0)
         gram = lax.psum(small_gram(sketch), "cam") / total_rows
         basis = apply_factor(gram, sketch)
         basis_low = basis.astype(jnp.bfloat16)

time: 1630 us -> 1550 us (0.951)
  waiting for transfers between devices: 481 us -> 387 us
    psum x2 -> x0, waiting for transfers between devices: 94.5 us -> none  [on_device(): sketch = lax.psum(partial_sketch, 'proj')]
    all_gather x0 -> x2, blocking collectives: none -> 25.3 us  [on_device(): sketch = jnp.sum(lax.all_gather(partial_sketch, 'proj'), axis=0)]
    unnamed x6 -> x4, waiting for transfers between devices: 386 us -> 387 us
  transfers between devices with their start and end apart: 4 -> 2, of which waited for: 4 -> 2; matrix products, arithmetic and copies ran while one was open for 0% -> 0% of each run, Pallas kernels for 0% -> 0%
where the time goes in v2:
time: 1550 us
  blocking collectives  1110 us (72%)
  waiting for transfers between devices  387 us (25%)
    psum x2, blocking collectives, on_device(): gram = lax.psum(small_gram(sketch), 'cam') / total_rows  982 us
    unnamed x4, waiting for transfers between devices  387 us
    all_gather x2, blocking collectives, on_device(): lax.all_gather(panel_piece, 'cam', axis=0, tiled=True)  107 us
  transfers between devices with their start and end apart: 2, of which 2 were waited for; matrix products, arithmetic and copies ran while one was open for 0% of the time, Pallas kernels for 0%

profile of v2, /device:TPU:2, one launch (start us, length us, event | category | flops | bytes accessed | tf_op | source)
XLA Modules:
  0.0 1547.9 jit_solution(13389474285750706124)
XLA Ops:
  7.2 0.0 reduce-scatter.7.cloned.1.call-start
  7.2 57.9 %all_gather.18 = bf16[4096,32]{1,0:T(8,128)(2,1)S(1)} all-gather(bf16[32,32]{1,0:T(8,128)(2,1)} %param.6), channel_id=1, replica_groups=mesh['cam'=128,'proj'=4] {'cam'}, dimensions={0}, use_global_device_ids=true | all-gather | bytes 264192 | tf_op jit(solution)/shard_map/all_gather | solution.py:29
  65.1 3.5 fusion.11
  68.6 12.6 all-gather
  81.2 0.2 reshape.12
  81.4 0.2 reduce_sum.18
  81.5 0.2 fusion.12
  81.7 490.9 %psum.14 = f32[32,32]{0,1:T(8,128)S(1)} all-reduce(f32[32,32]{0,1:T(8,128)S(1)} %fusion.12), channel_id=1, replica_groups=mesh['cam'=128,'proj'=4] {'cam'}, use_global_device_ids=true, to_apply=%region_1.0 | all-reduce | flops 1024 | bytes 8192 | tf_op jit(solution)/shard_map/psum | solution.py:33
  572.6 0.1 copy.10
  572.7 2.9 cholesky.44
  575.6 0.6 compare_reduce_fusion.1
  576.3 0.7 fusion.3
  576.9 2.4 custom-call.6
  579.4 0.3 convolution_convert_fusion
  579.7 3.0 convolution_bitcast_fusion.1
  582.7 2.0 copy.17
  584.7 0.0 reduce-scatter.7.cloned.1.call-update
  584.7 0.0 reduce-scatter.9.cloned.1.call-start
  584.7 193.5 %reduce-scatter.7.cloned.1.call-done = f32[32,32]{1,0:T(8,128)} async-done(((f32[4096,32]{1,0:T(8,128)}), f32[32,32]{1,0:T(8,128)}) %reduce-scatter.7.cloned.1.call-update) | async-done | bytes 4112
  778.2 0.8 copy.18
  779.0 0.1 copy.11
  779.1 49.0 %all_gather.21 = bf16[4096,32]{1,0:T(8,128)(2,1)S(1)} all-gather(bf16[32,32]{1,0:T(8,128)(2,1)S(1)} %copy.11), channel_id=1, replica_groups=mesh['cam'=128,'proj'=4] {'cam'}, dimensions={0}, use_global_device_ids=true | all-gather | bytes 264192 | tf_op jit(solution)/shard_map/all_gather | solution.py:29
  828.1 3.6 convolution_bitcast_fusion.3
  831.6 12.7 all-gather.1
  844.3 0.2 reshape.13
  844.5 0.2 reduce_sum.19
  844.7 0.2 fusion.13
  844.9 490.9 %psum.15 = f32[32,32]{0,1:T(8,128)S(1)} all-reduce(f32[32,32]{0,1:T(8,128)S(1)} %fusion.13), channel_id=1, replica_groups=mesh['cam'=128,'proj'=4] {'cam'}, use_global_device_ids=true, to_apply=%region_6.9 | all-reduce | flops 1024 | bytes 8192 | tf_op jit(solution)/shard_map/psum | solution.py:33
  1335.7 0.1 copy.13
  1335.8 2.9 cholesky.55
  1338.8 0.6 compare_reduce_fusion
  1339.4 0.7 fusion.4
  1340.1 2.4 custom-call.7
  1342.5 0.3 convolution_bitcast_fusion.2
  1342.8 0.0 copy-start
  1342.8 3.0 convolution_bitcast_fusion
  1345.8 2.0 copy.19
  1347.8 0.0 reduce-scatter.9.cloned.1.call-update
  1347.8 0.0 copy-done
  1347.9 193.2 %reduce-scatter.9.cloned.1.call-done = f32[32,32]{1,0:T(8,128)} async-done(((f32[4096,32]{1,0:T(8,128)}), f32[32,32]{1,0:T(8,128)}) %reduce-scatter.9.cloned.1.call-update) | async-done | bytes 4112
  (6 shorter events, 0.1 us)
Async XLA Ops:
  7.2 771.0 %reduce-scatter.7.cloned.1.call-start = ((), (), s32[]{:S(2)}) async-start(), calls=%async_computation.2 | async-start | bytes 2113536
  584.7 956.4 %reduce-scatter.9.cloned.1.call-start = ((), (), s32[]{:S(2)}) async-start(), calls=%async_computation.3 | async-start | bytes 2113536
  1342.8 5.0 copy-start
Sparse Core Ops, SparseCore 0:
  584.8 193.3 reduce-scatter.6
  1348.0 193.0 reduce-scatter.8
